TPU v7x, 32 devices: a whole 2x2x4 slice. The times are simulated.
32 devices in a mesh: dp: 2 (over x), layer: 4 (over y, core), tensor: 4 (over z).
Axes of the slice: x: 2, y: 2, z: 4, core: 2. Of those that a mesh axis runs over, the one named last changes fastest.
Arguments:
- embeddings: bfloat16 [256, 4096], P('dp', 'tensor'), may hold values from -180 to 180
- layer_weight: bfloat16 [8, 4096, 4096], P('layer', None, 'tensor'), may hold values from -0.09375 to 0.09375
- rotation: float32 [4096, 4096], P(('dp', 'layer'), 'tensor'), may hold values from -3.2 to 3.2
Outputs:
- updated_rotation: float32 [4096, 4096], P(('dp', 'layer'), 'tensor')
All inputs are finite; a program needn't handle non-finite values.
Results may differ from a plain program's by a relative error of at most 0.0042.
Values may be sent and summed in bfloat16 or wider, within the bound.
A program may use at most 128 MiB of HBM per device.

v0:
```python
import math

import jax
import jax.numpy as jnp
from jax import lax
from jax.sharding import PartitionSpec as P

D = 4096
MICRO = 4


def passed_along(value, axis, steps):
    count = lax.axis_size(axis)
    initial, last = (max(0, -steps), min(count, count - steps))
    return lax.ppermute(value, axis, [(source, source + steps) for source in range(initial, last)])


def normalize(hidden):
    widened = hidden.astype(jnp.float32)
    inverse = lax.rsqrt(jnp.mean(widened * widened, axis=-1, keepdims=True) + 1e-05)
    return (widened, (widened * inverse).astype(jnp.bfloat16))


def shards(embeddings, layer_weight, rotation):
    exact_mode = lax.Precision.HIGHEST
    root_width = math.sqrt(D)
    rotated = rotation / root_width
    panel = lax.all_gather(rotated, ("dp", "layer"), axis=0, tiled=True)
    section = lax.axis_index("layer")
    width = embeddings.shape[1]
    full_width = width * lax.axis_size("tensor")
    column_start = lax.axis_index("tensor") * width
    micro_rows = embeddings.shape[0] // MICRO
    section_layers = layer_weight.shape[0]
    steps_total = MICRO + lax.axis_size("layer") - 1

    def join_columns(shard):
        return lax.all_gather(shard, "tensor", axis=1, tiled=True)

    def run_section(hidden):
        records = []
        shard = None
        for level in range(section_layers):
            widened, normed = normalize(hidden)
            update = jnp.dot(normed, layer_weight[level], preferred_element_type=jnp.float32)
            own_part = lax.dynamic_slice_in_dim(widened, column_start, width, 1)
            shard = (own_part + update).astype(jnp.bfloat16)
            records.append(normed)
            if level + 1 < section_layers:
                hidden = join_columns(shard)
        return (shard, jnp.stack(records))

    def step_fn(step, carry):
        previous, records_all = carry
        position = step - section
        valid = (position >= 0) & (position < MICRO)
        slot_index = jnp.clip(position, 0, MICRO - 1)
        fresh = lax.dynamic_slice_in_dim(embeddings, slot_index * micro_rows, micro_rows, 0)
        incoming = jnp.where(section == 0, join_columns(fresh), previous)
        shard, records = run_section(incoming)
        current = lax.dynamic_slice_in_dim(records_all, slot_index, 1, 1)
        chosen = jnp.where(valid, records[:, None], current)
        records_all = lax.dynamic_update_slice_in_dim(records_all, chosen, slot_index, 1)
        passed = passed_along(join_columns(shard), "layer", 1)
        return (passed, records_all)

    start_state = jnp.zeros((micro_rows, full_width), jnp.bfloat16)
    records_zero = jnp.zeros((section_layers, MICRO, micro_rows, full_width), jnp.bfloat16)
    final_state, records_all = lax.fori_loop(0, steps_total, step_fn, (start_state, records_zero))
    activations = records_all.reshape(-1, full_width)
    projected = jnp.dot(activations.astype(jnp.float32), panel, precision=exact_mode)
    cubed = projected * projected * projected
    columns = activations.astype(jnp.float32)
    summed = lax.psum_scatter(
        lax.dot_general(columns, cubed, (((0,), (0,)), ((), ())), precision=exact_mode),
        ("dp", "layer"),
        scatter_dimension=0,
        tiled=True,
    )
    gradient = summed / (embeddings.shape[0] * lax.axis_size("dp"))
    cross = lax.dot_general(gradient, panel, (((1,), (1,)), ((), ())), precision=exact_mode)
    cross_rows = lax.psum(cross, "tensor")
    swapped = lax.all_to_all(cross_rows, ("dp", "layer"), split_axis=1, concat_axis=0, tiled=True)
    skew_rows = cross_rows - swapped.T
    square_total = lax.psum(jnp.sum(skew_rows * skew_rows), ("dp", "layer"))
    mean_square = square_total / (full_width * full_width)
    step_size = 0.5 / jnp.sqrt(full_width * (mean_square + 1e-06))
    first_product = jnp.dot(skew_rows, panel, precision=exact_mode)
    first_guess = rotated - step_size * first_product
    second_product = jnp.dot(
        skew_rows,
        lax.all_gather(first_guess, ("dp", "layer"), axis=0, tiled=True),
        precision=exact_mode,
    )
    refined = rotated - 0.5 * step_size * (first_product + second_product)
    return root_width * refined


def solution(mesh):
    return jax.shard_map(
        shards,
        mesh=mesh,
        in_specs=(P("dp", "tensor"), P("layer", None, "tensor"), P(("dp", "layer"), "tensor")),
        out_specs=P(("dp", "layer"), "tensor"),
        check_vma=False,
    )
```

profile of v0, /device:TPU:0, one launch (start us, length us, event | category | flops | bytes accessed | tf_op | source)
XLA Modules:
  0.0 1216.2 jit_solution(3677848573825620444)
XLA Ops:
  10.1 428.7 %while.17 = (s32[]{:T(128)}, bf16[32,4096]{1,0:T(8,128)(2,1)S(1)}, bf16[2,4,32,4096]{3,2,1,0:T(8,128)(2,1)S(1)}, pred[]{:T(512)}, s32[]{:T(128)}, /*index=5*/bf1...) while((s32[]{:T(128)}, bf16[32,4096]{1,0:T(8,128)(2,1)S(1)}, ...), condition=%wide.region_3.4_spmd, body=%wide.region_0.3_spmd.sunk | while | flops 541065280 | bytes 26151456 | solution.py:69
  11.0 15.6 %all_gather.38 = bf16[32,4096]{1,0:T(8,128)(2,1)S(1)} all-gather(bf16[32,1024]{1,0:T(8,128)(2,1)S(1)} %constant_dynamic-slice_fusion.4), channel_id=1, replica_groups=mesh['dp'=2,'layer'=4,'tensor'=4] {'tensor'}, dimensions={1}, use_global_device_ids=true | all-gather | bytes 327680 | tf_op jit(solution)/shard_map/while/body/eval_jaxpr/all_gather | solution.py:38
  31.9 14.4 %all_gather.39 = bf16[32,4096]{1,0:T(8,128)(2,1)S(1)} all-gather(bf16[32,1024]{1,0:T(8,128)(2,1)S(1)} %fusion.45), channel_id=1, replica_groups=mesh['dp'=2,'layer'=4,'tensor'=4] {'tensor'}, dimensions={1}, use_global_device_ids=true | all-gather | bytes 327680 | tf_op jit(solution)/shard_map/while/body/eval_jaxpr/all_gather | solution.py:38
  46.5 5.0 fusion.46
  51.5 15.1 %all_gather.40 = bf16[32,4096]{1,0:T(8,128)(2,1)} all-gather(bf16[32,1024]{1,0:T(8,128)(2,1)S(1)} %fusion.46), channel_id=1, replica_groups=mesh['dp'=2,'layer'=4,'tensor'=4] {'tensor'}, dimensions={1}, use_global_device_ids=true | all-gather | bytes 327680 | tf_op jit(solution)/shard_map/while/body/eval_jaxpr/all_gather | solution.py:38
  70.2 13.9 %all_gather.38 = bf16[32,4096]{1,0:T(8,128)(2,1)S(1)} all-gather(bf16[32,1024]{1,0:T(8,128)(2,1)S(1)} %constant_dynamic-slice_fusion.4), channel_id=1, replica_groups=mesh['dp'=2,'layer'=4,'tensor'=4] {'tensor'}, dimensions={1}, use_global_device_ids=true | all-gather | bytes 327680 | tf_op jit(solution)/shard_map/while/body/eval_jaxpr/all_gather | solution.py:38
  84.4 5.0 fusion.45
  89.4 13.9 %all_gather.39 = bf16[32,4096]{1,0:T(8,128)(2,1)S(1)} all-gather(bf16[32,1024]{1,0:T(8,128)(2,1)S(1)} %fusion.45), channel_id=1, replica_groups=mesh['dp'=2,'layer'=4,'tensor'=4] {'tensor'}, dimensions={1}, use_global_device_ids=true | all-gather | bytes 327680 | tf_op jit(solution)/shard_map/while/body/eval_jaxpr/all_gather | solution.py:38
  103.5 5.0 fusion.46
  108.5 15.2 %all_gather.40 = bf16[32,4096]{1,0:T(8,128)(2,1)} all-gather(bf16[32,1024]{1,0:T(8,128)(2,1)S(1)} %fusion.46), channel_id=1, replica_groups=mesh['dp'=2,'layer'=4,'tensor'=4] {'tensor'}, dimensions={1}, use_global_device_ids=true | all-gather | bytes 327680 | tf_op jit(solution)/shard_map/while/body/eval_jaxpr/all_gather | solution.py:38
  129.2 13.9 %all_gather.38 = bf16[32,4096]{1,0:T(8,128)(2,1)S(1)} all-gather(bf16[32,1024]{1,0:T(8,128)(2,1)S(1)} %constant_dynamic-slice_fusion.4), channel_id=1, replica_groups=mesh['dp'=2,'layer'=4,'tensor'=4] {'tensor'}, dimensions={1}, use_global_device_ids=true | all-gather | bytes 327680 | tf_op jit(solution)/shard_map/while/body/eval_jaxpr/all_gather | solution.py:38
  143.3 5.0 fusion.45
  148.3 14.0 %all_gather.39 = bf16[32,4096]{1,0:T(8,128)(2,1)S(1)} all-gather(bf16[32,1024]{1,0:T(8,128)(2,1)S(1)} %fusion.45), channel_id=1, replica_groups=mesh['dp'=2,'layer'=4,'tensor'=4] {'tensor'}, dimensions={1}, use_global_device_ids=true | all-gather | bytes 327680 | tf_op jit(solution)/shard_map/while/body/eval_jaxpr/all_gather | solution.py:38
  162.5 5.0 fusion.46
  167.5 14.6 %all_gather.40 = bf16[32,4096]{1,0:T(8,128)(2,1)} all-gather(bf16[32,1024]{1,0:T(8,128)(2,1)S(1)} %fusion.46), channel_id=1, replica_groups=mesh['dp'=2,'layer'=4,'tensor'=4] {'tensor'}, dimensions={1}, use_global_device_ids=true | all-gather | bytes 327680 | tf_op jit(solution)/shard_map/while/body/eval_jaxpr/all_gather | solution.py:38
  182.2 7.4 collective-permute-start
  191.7 13.8 %all_gather.38 = bf16[32,4096]{1,0:T(8,128)(2,1)S(1)} all-gather(bf16[32,1024]{1,0:T(8,128)(2,1)S(1)} %constant_dynamic-slice_fusion.4), channel_id=1, replica_groups=mesh['dp'=2,'layer'=4,'tensor'=4] {'tensor'}, dimensions={1}, use_global_device_ids=true | all-gather | bytes 327680 | tf_op jit(solution)/shard_map/while/body/eval_jaxpr/all_gather | solution.py:38
  210.8 13.8 %all_gather.39 = bf16[32,4096]{1,0:T(8,128)(2,1)S(1)} all-gather(bf16[32,1024]{1,0:T(8,128)(2,1)S(1)} %fusion.45), channel_id=1, replica_groups=mesh['dp'=2,'layer'=4,'tensor'=4] {'tensor'}, dimensions={1}, use_global_device_ids=true | all-gather | bytes 327680 | tf_op jit(solution)/shard_map/while/body/eval_jaxpr/all_gather | solution.py:38
  229.8 14.5 %all_gather.40 = bf16[32,4096]{1,0:T(8,128)(2,1)} all-gather(bf16[32,1024]{1,0:T(8,128)(2,1)S(1)} %fusion.46), channel_id=1, replica_groups=mesh['dp'=2,'layer'=4,'tensor'=4] {'tensor'}, dimensions={1}, use_global_device_ids=true | all-gather | bytes 327680 | tf_op jit(solution)/shard_map/while/body/eval_jaxpr/all_gather | solution.py:38
  244.3 6.7 collective-permute-start
  253.2 13.8 %all_gather.38 = bf16[32,4096]{1,0:T(8,128)(2,1)S(1)} all-gather(bf16[32,1024]{1,0:T(8,128)(2,1)S(1)} %constant_dynamic-slice_fusion.4), channel_id=1, replica_groups=mesh['dp'=2,'layer'=4,'tensor'=4] {'tensor'}, dimensions={1}, use_global_device_ids=true | all-gather | bytes 327680 | tf_op jit(solution)/shard_map/while/body/eval_jaxpr/all_gather | solution.py:38
  267.2 5.0 fusion.45
  272.2 13.8 %all_gather.39 = bf16[32,4096]{1,0:T(8,128)(2,1)S(1)} all-gather(bf16[32,1024]{1,0:T(8,128)(2,1)S(1)} %fusion.45), channel_id=1, replica_groups=mesh['dp'=2,'layer'=4,'tensor'=4] {'tensor'}, dimensions={1}, use_global_device_ids=true | all-gather | bytes 327680 | tf_op jit(solution)/shard_map/while/body/eval_jaxpr/all_gather | solution.py:38
  291.3 14.5 %all_gather.40 = bf16[32,4096]{1,0:T(8,128)(2,1)} all-gather(bf16[32,1024]{1,0:T(8,128)(2,1)S(1)} %fusion.46), channel_id=1, replica_groups=mesh['dp'=2,'layer'=4,'tensor'=4] {'tensor'}, dimensions={1}, use_global_device_ids=true | all-gather | bytes 327680 | tf_op jit(solution)/shard_map/while/body/eval_jaxpr/all_gather | solution.py:38
  305.8 7.3 collective-permute-start
  315.3 13.9 %all_gather.38 = bf16[32,4096]{1,0:T(8,128)(2,1)S(1)} all-gather(bf16[32,1024]{1,0:T(8,128)(2,1)S(1)} %constant_dynamic-slice_fusion.4), channel_id=1, replica_groups=mesh['dp'=2,'layer'=4,'tensor'=4] {'tensor'}, dimensions={1}, use_global_device_ids=true | all-gather | bytes 327680 | tf_op jit(solution)/shard_map/while/body/eval_jaxpr/all_gather | solution.py:38
  329.5 5.0 fusion.45
  334.5 13.8 %all_gather.39 = bf16[32,4096]{1,0:T(8,128)(2,1)S(1)} all-gather(bf16[32,1024]{1,0:T(8,128)(2,1)S(1)} %fusion.45), channel_id=1, replica_groups=mesh['dp'=2,'layer'=4,'tensor'=4] {'tensor'}, dimensions={1}, use_global_device_ids=true | all-gather | bytes 327680 | tf_op jit(solution)/shard_map/while/body/eval_jaxpr/all_gather | solution.py:38
  348.5 5.0 fusion.46
  353.5 14.5 %all_gather.40 = bf16[32,4096]{1,0:T(8,128)(2,1)} all-gather(bf16[32,1024]{1,0:T(8,128)(2,1)S(1)} %fusion.46), channel_id=1, replica_groups=mesh['dp'=2,'layer'=4,'tensor'=4] {'tensor'}, dimensions={1}, use_global_device_ids=true | all-gather | bytes 327680 | tf_op jit(solution)/shard_map/while/body/eval_jaxpr/all_gather | solution.py:38
  368.1 7.2 collective-permute-start
  377.5 13.9 %all_gather.38 = bf16[32,4096]{1,0:T(8,128)(2,1)S(1)} all-gather(bf16[32,1024]{1,0:T(8,128)(2,1)S(1)} %constant_dynamic-slice_fusion.4), channel_id=1, replica_groups=mesh['dp'=2,'layer'=4,'tensor'=4] {'tensor'}, dimensions={1}, use_global_device_ids=true | all-gather | bytes 327680 | tf_op jit(solution)/shard_map/while/body/eval_jaxpr/all_gather | solution.py:38
  396.7 13.8 %all_gather.39 = bf16[32,4096]{1,0:T(8,128)(2,1)S(1)} all-gather(bf16[32,1024]{1,0:T(8,128)(2,1)S(1)} %fusion.45), channel_id=1, replica_groups=mesh['dp'=2,'layer'=4,'tensor'=4] {'tensor'}, dimensions={1}, use_global_device_ids=true | all-gather | bytes 327680 | tf_op jit(solution)/shard_map/while/body/eval_jaxpr/all_gather | solution.py:38
  415.7 14.5 %all_gather.40 = bf16[32,4096]{1,0:T(8,128)(2,1)} all-gather(bf16[32,1024]{1,0:T(8,128)(2,1)S(1)} %fusion.46), channel_id=1, replica_groups=mesh['dp'=2,'layer'=4,'tensor'=4] {'tensor'}, dimensions={1}, use_global_device_ids=true | all-gather | bytes 327680 | tf_op jit(solution)/shard_map/while/body/eval_jaxpr/all_gather | solution.py:38
  430.2 7.2 collective-permute-start
  438.8 12.0 fusion.29
  450.8 10.4 fusion.25
  461.4 131.6 %reduce-scatter.2.cloned.1.call-done = f32[512,1024]{1,0:T(8,128)} async-done(((f32[4096,1024]{1,0:T(8,128)}), f32[512,1024]{1,0:T(8,128)}) %reduce-scatter.2.cloned.1.call-update) | async-done | bytes 2097168 | tf_op jit(solution)/shard_map/reduce_scatter | solution.py:74
  593.0 31.8 %fusion.23 = f32[512,4096]{1,0:T(8,128)} fusion(f32[4096,1024]{1,0:T(8,128)} %all-gather.3.cloned.1.call-done, f32[512,1024]{1,0:T(8,128)} %reduce-scatter.2.cloned.1.call-done), kind=kOutput, calls=%fused_computation.29 | convolution fusion | flops 25770328064 | bytes 27262976 | tf_op jit(solution)/shard_map/dot_general | solution.py:81
  624.9 290.9 %all-reduce.2.cloned.1.call-done = f32[512,4096]{1,0:T(8,128)} async-done(((f32[512,4096]{1,0:T(8,128)}), f32[512,4096]{1,0:T(8,128)}) %all-reduce.2.cloned.1.call-update) | async-done | bytes 8388624 | tf_op jit(solution)/shard_map/psum | solution.py:82
  915.8 9.0 copy.10
  924.8 100.4 %all_to_all.19 = f32[512,8,512]{0,2,1:T(8,128)} all-to-all(f32[512,8,512]{0,2,1:T(8,128)} %bitcast.73), channel_id=1, replica_groups=mesh['dp'=2,'layer'=4,'tensor'=4] {'dp','layer'}, dimensions={1} | all-to-all | bytes 16777216 | tf_op jit(solution)/shard_map/all_to_all | solution.py:83
  1025.2 8.2 copy.14
  1033.4 6.3 multiply_reduce_fusion.2
  1039.7 13.2 %psum.15 = f32[]{:T(128)} all-reduce(f32[]{:T(128)} %multiply_reduce_fusion.2), channel_id=1, replica_groups=mesh['dp'=2,'layer'=4,'tensor'=4] {'dp','layer'}, use_global_device_ids=true, to_apply=%region_7.8 | all-reduce | flops 1 | bytes 8 | tf_op jit(solution)/shard_map/psum | solution.py:85
  1053.6 33.4 %multiply_subtract_fusion = (f32[512,1024]{1,0:T(8,128)}, f32[512,1024]{1,0:T(8,128)}) fusion(f32[]{:T(128)S(6)} %div.29, f32[512,1024]{1,0:T(8,128)S(1)} %copy-done, f32[4096,1024]{1,0:T(8,128)} %all-gather.3.cloned.1.call-done, f32[512,4096]{1,0:T(8,128)} %all-reduce.2.cloned.1.call-done, f32[4096,512]{0,1:T(8,128)} %bitcast.68), kind=kOutput, calls=%fused_computation.28 | convolution fusion | flops 25773473792 | bytes 39845892 | tf_op jit(solution)/shard_map/dot_general | solution.py:88
  1087.0 88.1 %all-gather.5.cloned.1.call-done = f32[4096,1024]{1,0:T(8,128)} async-done(((f32[512,1024]{1,0:T(8,128)}), f32[4096,1024]{1,0:T(8,128)}) %all-gather.5.cloned.1.call-update) | async-done | bytes 16777232 | tf_op jit(solution)/shard_map/all_gather | solution.py:92
  1175.1 34.5 %subtract_multiply_fusion = f32[512,1024]{1,0:T(8,128)} fusion(f32[512,1024]{1,0:T(8,128)} %get-tuple-element.203, f32[4096,1024]{1,0:T(8,128)} %all-gather.5.cloned.1.call-done, f32[]{:T(128)S(6)} %mul.119, f32[512,1024]{1,0:T(8,128)S(1)} %copy-done, f32[512,4096]{1,0:T(8,128)} %all-reduce.2.cloned.1.call-done, f32[4096,512]{0,1:T(8,128)} %bitcast.69), kind=kOutput, calls=%fused_computation.27 | convolution fusion | flops 25774522368 | bytes 39845892 | tf_op jit(solution)/shard_map/dot_general | solution.py:90
  (111 shorter events, 56.7 us)
Async XLA Ops:
  6.5 432.3 %all-gather.3.cloned.1.call-start = ((), (), s32[]{:S(2)}) async-start(), calls=%async_computation.2 | async-start | bytes 18874368 | tf_op jit(solution)/shard_map/all_gather | solution.py:28
  9.8 583.2 %reduce-scatter.2.cloned.1.call-start = ((), (), s32[]{:S(2)}) async-start(), calls=%async_computation.3 | async-start | bytes 18874368 | tf_op jit(solution)/shard_map/reduce_scatter | solution.py:74
  66.7 2.7 collective-permute-start
  123.7 4.6 collective-permute-start
  182.2 8.7 collective-permute-start
  244.3 8.0 collective-permute-start
  305.8 8.7 collective-permute-start
  368.1 8.6 collective-permute-start
  430.2 8.6 collective-permute-start
  461.2 454.6 %all-reduce.2.cloned.1.call-start = ((), (), s32[]{:S(2)}) async-start(), calls=%async_computation.4 | async-start | bytes 16777216 | tf_op jit(solution)/shard_map/psum | solution.py:82
  624.8 550.3 %all-gather.5.cloned.1.call-start = ((), (), s32[]{:S(2)}) async-start(), calls=%async_computation.5 | async-start | bytes 18874368 | tf_op jit(solution)/shard_map/all_gather | solution.py:92
  924.8 108.6 %slice-start = ((s8[8388608]{0:T(1024)(128)(4,1)}), s8[4194304]{0:T(1024)(128)(4,1)S(1)}, s32[]{:S(2)}) async-start(s8[8388608]{0:T(1024)(128)(4,1)} %bitcast.65), calls=%async_computation.6 | async-start | bytes 8388608
  1025.2 8.2 slice-start.1
  1033.4 20.2 %copy-start = (f32[512,1024]{1,0:T(8,128)S(1)}, f32[512,1024]{1,0:T(8,128)}, u32[]{:S(2)}) copy-start(f32[512,1024]{1,0:T(8,128)} %param.7) | copy-start | bytes 6291460
Sparse Core Ops, SparseCore 0:
  9.9 92.6 all-gather.2
  461.3 131.6 reduce-scatter.1
  625.0 290.8 all-reduce.1
  1087.1 87.9 all-gather.4
where the time goes:
time: 1220 us
  waiting for transfers between devices  517 us (42%)
  blocking collectives  413 us (34%)
  matrix products  192 us (16%)
  starting transfers between devices  40.8 us (3%)
  local copies, waits for them, and re-layouts  23.7 us (2%)
  other arithmetic  15.3 us (1%)
  between operations  13.9 us (1%)
    all_gather x21, blocking collectives, join_columns(): return lax.all_gather(shard, 'tensor', axis=1, tiled=True)  299 us
    psum x1, waiting for transfers between devices, shards(): cross_rows = lax.psum(cross, 'tensor')  291 us
    reduce_scatter x1, waiting for transfers between devices, shards(): lax.psum_scatter(lax.dot_general(columns, cubed, (((0,), (0,)), ((), ()))...  132 us
    all_to_all x1, blocking collectives, shards(): lax.all_to_all(cross_rows, ('dp', 'layer'), split_axis=1, concat_axis=0,...  100 us
    all_gather x1, waiting for transfers between devices, shards(): lax.all_gather(first_guess, ('dp', 'layer'), axis=0, tiled=True)  88.1 us
    dot_general x14, matrix products, run_section(): jnp.dot(normed, layer_weight[level], preferred_element_type=jnp.float32)  69.8 us
    ppermute x7, starting transfers between devices, passed_along(): lax.ppermute(value, axis, [(source, source + steps) for source in range(i...  40.5 us
    dot_general x1, matrix products, shards(): jnp.dot(skew_rows, lax.all_gather(first_guess, ('dp', 'layer'), axis=0, t...  34.5 us
  transfers between devices with their start and end apart: 11, of which 10 were waited for; matrix products, arithmetic and copies ran while one was open for 7% of the time, Pallas kernels for 0%

commit v1 on v0

v1 whole, which is shorter than its diff:
```python
import functools
import math

import jax
import jax.numpy as jnp
from jax import lax
from jax.experimental import pallas as pl
from jax.experimental.pallas import tpu as pltpu
from jax.sharding import PartitionSpec as P

ROWS = ("dp", "layer")
EVERY = ("dp", "layer", "tensor")
HALF = jnp.bfloat16
CHUNKS = 2
MESH = pl.DeviceIdType.MESH


def product(left, right, left_dim, right_dim):
    dims = (((left_dim,), (right_dim,)), ((), ()))
    return lax.dot_general(left.astype(HALF), right.astype(HALF), dims, preferred_element_type=jnp.float32)


def split(value):
    head = lax.reduce_precision(value, 8, 7)
    return head.astype(HALF), (value - head).astype(HALF)


def layers_kernel(chunks, embeddings, weight_hbm, records, hidden, outbox, weight, send_sem, recv_sem, weight_sem):
    dp, section, me = (lax.axis_index(name) for name in EVERY)
    sections, columns = lax.axis_size("layer"), lax.axis_size("tensor")
    levels = weight_hbm.shape[0]
    width = embeddings.shape[1]
    rows = embeddings.shape[0] // chunks
    tile = min(256, width)

    loads = [
        pltpu.make_async_copy(weight_hbm.at[level], weight.at[level], weight_sem.at[level])
        for level in range(levels)
    ]
    for load in loads:
        load.start()

    barrier = pltpu.get_barrier_semaphore()

    def greet(row, column):
        pl.semaphore_signal(barrier, inc=1, device_id=(dp, row, column), device_id_type=MESH)

    for column in range(columns):
        pl.when(column != me)(lambda column=column: greet(section, column))
        pl.when(section > 0)(lambda column=column: greet(section - 1, column))
        pl.when(section + 1 < sections)(lambda column=column: greet(section + 1, column))
    edges = jnp.where(section > 0, 1, 0) + jnp.where(section + 1 < sections, 1, 0)
    pl.semaphore_wait(barrier, columns - 1 + columns * edges)

    def copy(stage, chunk, source, column):
        level, row = (stage, section) if stage < levels else (0, section + 1)
        return pltpu.make_async_remote_copy(
            src_ref=source,
            dst_ref=hidden.at[level, chunk, me],
            send_sem=send_sem.at[stage, chunk, column],
            recv_sem=recv_sem.at[level, chunk, me],
            device_id=(dp, row, column),
            device_id_type=MESH,
        )

    def source_of(stage, chunk):
        return hidden.at[stage, chunk, me] if stage < levels else outbox.at[chunk]

    def sends(stage, chunk, action):
        for column in range(columns):
            if stage == 0:
                wanted = (section == 0) & (column != me)
            elif stage < levels:
                wanted = column != me
            else:
                wanted = section + 1 < sections
            pl.when(wanted)(lambda column=column: action(copy(stage, chunk, source_of(stage, chunk), column)))

    def arrivals(level, chunk):
        for column in range(columns):
            wanted = column != me
            if level == 0:
                wanted = wanted | (section > 0)

            @pl.when(wanted)
            def _():
                pltpu.make_async_remote_copy(
                    src_ref=hidden.at[level, chunk, column],
                    dst_ref=hidden.at[level, chunk, column],
                    send_sem=send_sem.at[level, chunk, column],
                    recv_sem=recv_sem.at[level, chunk, column],
                    device_id=(dp, section, column),
                    device_id_type=MESH,
                ).wait_recv()

    for chunk in range(chunks):

        @pl.when(section == 0)
        def _():
            hidden[0, chunk, me] = embeddings[chunk * rows : (chunk + 1) * rows, :]

        sends(0, chunk, lambda one: one.start())

    for level in range(levels):
        for chunk in range(chunks):
            arrivals(level, chunk)
            total = jnp.zeros((rows, 1), jnp.float32)
            for column in range(columns):
                widened = hidden[level, chunk, column].astype(jnp.float32)
                total = total + jnp.sum(widened * widened, axis=-1, keepdims=True)
            inverse = lax.rsqrt(total / (columns * width) + 1e-05)
            for column in range(columns):
                widened = hidden[level, chunk, column].astype(jnp.float32)
                records[level, chunk, :, column * width : (column + 1) * width] = (widened * inverse).astype(HALF)
            if chunk == 0:
                loads[level].wait()

            def multiply(part, _):
                place = pl.ds(pl.multiple_of(part * tile, tile), tile)
                update = jnp.dot(
                    records[level, chunk], weight[level, :, place], preferred_element_type=jnp.float32
                )
                fresh = (hidden[level, chunk, me, :, place].astype(jnp.float32) + update).astype(HALF)
                if level + 1 < levels:
                    hidden[level + 1, chunk, me, :, place] = fresh
                else:
                    outbox[chunk, :, place] = fresh
                return 0

            lax.fori_loop(0, width // tile, multiply, 0)
            sends(level + 1, chunk, lambda one: one.start())
    for stage in range(levels + 1):
        for chunk in range(chunks):
            sends(stage, chunk, lambda one: one.wait_send())


def run_layers(embeddings, layer_weight):
    levels, full, width = layer_weight.shape
    tokens = embeddings.shape[0]
    columns = lax.axis_size("tensor")
    rows = tokens // CHUNKS
    records = pl.pallas_call(
        functools.partial(layers_kernel, CHUNKS),
        out_shape=jax.ShapeDtypeStruct((levels, CHUNKS, rows, full), HALF),
        in_specs=[pl.BlockSpec(memory_space=pltpu.VMEM), pl.BlockSpec(memory_space=pl.ANY)],
        out_specs=pl.BlockSpec(memory_space=pltpu.VMEM),
        scratch_shapes=[
            pltpu.VMEM((levels, CHUNKS, columns, rows, width), HALF),
            pltpu.VMEM((CHUNKS, rows, width), HALF),
            pltpu.VMEM((levels, full, width), HALF),
            pltpu.SemaphoreType.DMA((levels + 1, CHUNKS, columns)),
            pltpu.SemaphoreType.DMA((levels, CHUNKS, columns)),
            pltpu.SemaphoreType.DMA((levels,)),
        ],
        compiler_params=pltpu.CompilerParams(
            collective_id=0, has_side_effects=True, vmem_limit_bytes=40 * 1024 * 1024
        ),
        cost_estimate=pl.CostEstimate(
            flops=2 * tokens * full * width * levels * 40,
            bytes_accessed=layer_weight.size * 2 * 20,
            transcendentals=0,
        ),
    )(embeddings, layer_weight)
    return records.reshape(levels * tokens, full)


def transposed_block(block):
    row_groups = lax.axis_size("dp") * lax.axis_size("layer")
    columns = lax.axis_size("tensor")
    share = row_groups // columns
    side = block.shape[0]
    own = lax.axis_index(ROWS) % share
    result = jnp.zeros_like(block)
    for turn in range(share):
        pairs = []
        for i in range(row_groups):
            for t in range(columns):
                part = (i + turn) % share
                pairs.append((i * columns + t, (share * t + part) * columns + i // share))
        piece = lax.dynamic_slice_in_dim(block, ((own + turn) % share) * side, side, 1)
        got = lax.ppermute(piece, EVERY, pairs)
        place = (own + share - turn) % share
        result = lax.dynamic_update_slice_in_dim(result, got.T, place * side, 1)
    return result


def shards(embeddings, layer_weight, rotation):
    full_width = layer_weight.shape[1]
    root_width = math.sqrt(full_width)
    rotated = rotation / root_width
    panel, panel_rest = (lax.all_gather(part, ROWS, axis=0, tiled=True) for part in split(rotated))
    activations = run_layers(embeddings, layer_weight)
    projected = product(activations, panel, 1, 0) + product(activations, panel_rest, 1, 0)
    cubed = projected * projected * projected
    partial = product(activations, cubed, 0, 0).astype(HALF)
    summed = lax.psum_scatter(partial, ROWS, scatter_dimension=0, tiled=True)
    gradient = summed.astype(jnp.float32) / (embeddings.shape[0] * lax.axis_size("dp"))
    cross_part = (product(gradient, panel, 1, 1) + product(gradient, panel_rest, 1, 1)).astype(HALF)
    cross = lax.psum_scatter(cross_part, "tensor", scatter_dimension=1, tiled=True)
    skew = cross.astype(jnp.float32) - transposed_block(cross).astype(jnp.float32)
    skew_rows = lax.all_gather(skew.astype(HALF), "tensor", axis=1, tiled=True)
    first_product = product(skew_rows, panel, 1, 0)
    product_panel = lax.all_gather(first_product.astype(HALF), ROWS, axis=0, tiled=True)
    square_total = lax.psum(jnp.sum(skew * skew), EVERY)
    mean_square = square_total / (full_width * full_width)
    step_size = 0.5 / jnp.sqrt(full_width * (mean_square + 1e-06))
    second_product = product(skew_rows, product_panel, 1, 0)
    refined = rotated - step_size * first_product + (0.5 * step_size * step_size) * second_product
    return root_width * refined


def solution(mesh):
    return jax.shard_map(
        shards,
        mesh=mesh,
        in_specs=(P("dp", "tensor"), P("layer", None, "tensor"), P(("dp", "layer"), "tensor")),
        out_specs=P(("dp", "layer"), "tensor"),
        check_vma=False,
    )
```

time: 1220 us -> 555 us (0.45)
  blocking collectives: 413 us -> 39.6 us
  matrix products: 192 us -> 61.3 us
  waiting for transfers between devices: 517 us -> 393 us
  starting transfers between devices: 40.8 us -> 1.15 us
  Pallas kernels: 0 us -> 37 us
  local copies, waits for them, and re-layouts: 23.7 us -> 2.81 us
    all_gather x21 -> x0, blocking collectives: 299 us -> none  [join_columns(): return lax.all_gather(shard, 'tensor', axis=1, tiled=True)]
    psum x1 -> x0, waiting for transfers between devices: 291 us -> none  [shards(): cross_rows = lax.psum(cross, 'tensor')]
    all_gather x2 -> x4, waiting for transfers between devices: 88.1 us -> 243 us  [the longest x1 150 us: shards(): skew_rows = lax.all_gather(skew.astype(HALF), 'tensor', axis=1, tiled=True)]
    dot_general x19 -> x7, matrix products: 192 us -> 61.3 us  [product(): lax.dot_general(left.astype(HALF), right.astype(HALF), dims, preferred_el...]
    all_to_all x1 -> x0, blocking collectives: 100 us -> none  [shards(): lax.all_to_all(cross_rows, ('dp', 'layer'), split_axis=1, concat_axis=0,...]
    ppermute x7 -> x2, starting transfers between devices: 40.5 us -> 0.77 us  [transposed_block(): got = lax.ppermute(piece, EVERY, pairs)]
    pallas_call x0 -> x1, Pallas kernels: none -> 37 us  [run_layers(): pl.pallas_call(functools.partial(layers_kernel, CHUNKS), out_shape=jax.Sh...]
    psum x1, blocking collectives: 13.2 us -> 39.6 us  [shards(): square_total = lax.psum(jnp.sum(skew * skew), EVERY)]
  transfers between devices with their start and end apart: 11 -> 8, of which waited for: 10 -> 7; matrix products, arithmetic and copies ran while one was open for 7% -> 1% of each run, Pallas kernels for 0% -> 7%
where the time goes in v1:
time: 555 us
  waiting for transfers between devices  393 us (71%)
  matrix products  61.3 us (11%)
  blocking collectives  39.6 us (7%)
  Pallas kernels  37 us (7%)
  between operations  14.3 us (3%)
    all_gather x1, waiting for transfers between devices, shards(): skew_rows = lax.all_gather(skew.astype(HALF), 'tensor', axis=1, tiled=True)  150 us
    all_gather x2, waiting for transfers between devices, shards(): lax.all_gather(part, ROWS, axis=0, tiled=True)  79.5 us
    reduce_scatter x1, waiting for transfers between devices, shards(): lax.psum_scatter(cross_part, 'tensor', scatter_dimension=1, tiled=True)  76.8 us
    reduce_scatter x1, waiting for transfers between devices, shards(): summed = lax.psum_scatter(partial, ROWS, scatter_dimension=0, tiled=True)  71.2 us
    dot_general x7, matrix products, product(): lax.dot_general(left.astype(HALF), right.astype(HALF), dims, preferred_el...  61.3 us
    psum x1, blocking collectives, shards(): square_total = lax.psum(jnp.sum(skew * skew), EVERY)  39.6 us
    pallas_call x1, Pallas kernels, run_layers(): pl.pallas_call(functools.partial(layers_kernel, CHUNKS), out_shape=jax.Sh...  37 us
    all_gather x1, waiting for transfers between devices, shards(): lax.all_gather(first_product.astype(HALF), ROWS, axis=0, tiled=True)  13.6 us
  transfers between devices with their start and end apart: 8, of which 7 were waited for; matrix products, arithmetic and copies ran while one was open for 1% of the time, Pallas kernels for 7%

profile of v1, /device:TPU:0, one launch (start us, length us, event | category | flops | bytes accessed | tf_op | source)
XLA Modules:
  0.0 554.8 jit_solution(7827723478128896015)
XLA Ops:
  6.5 0.0 all-gather.5.cloned.1.call-start
  6.5 3.4 fusion
  9.9 0.0 copy-start
  9.9 0.0 all-gather.5.cloned.1.call-update
  9.9 0.0 all-gather.7.cloned.1.call-start
  10.0 0.7 all-gather.7.cloned.1.call-update
  10.7 0.0 reduce-scatter.3.cloned.1.call-start
  10.7 0.1 copy-done
  10.8 37.0 %shard_map.37 = bf16[2,2,64,4096]{3,2,1,0:T(8,128)(2,1)S(1)} custom-call(bf16[128,1024]{1,0:T(8,128)(2,1)S(1)} %copy-done, bf16[2,4096,1024]{2,1,0:T(8,128)(2,1)} %weight_hbm.1), custom_call_target="tpu_custom_call" | custom-call | flops 85899345920 | bytes 335544320 | tf_op jit(solution)/shard_map/pallas_call | solution.py:142
  47.8 22.7 %all-gather.5.cloned.1.call-done = bf16[4096,1024]{1,0:T(8,128)(2,1)} async-done(((bf16[512,1024]{1,0:T(8,128)(2,1)}), bf16[4096,1024]{1,0:T(8,128)(2,1)}) %all-gather.5.cloned.1.call-update) | async-done | bytes 8388624 | tf_op jit(solution)/shard_map/all_gather | solution.py:191
  70.6 5.7 %fusion.7 = f32[256,1024]{1,0:T(8,128)S(1)} fusion(bf16[256,4096]{1,0:T(8,128)(2,1)S(1)} %bitcast.15, bf16[4096,1024]{1,0:T(8,128)(2,1)} %all-gather.5.cloned.1.call-done), kind=kOutput, calls=%fused_computation.21 | convolution fusion | flops 2147483648 | bytes 11534336 | tf_op jit(solution)/shard_map/dot_general | solution.py:20
  76.3 56.7 %all-gather.7.cloned.1.call-done = bf16[4096,1024]{1,0:T(8,128)(2,1)} async-done(((bf16[512,1024]{1,0:T(8,128)(2,1)}), bf16[4096,1024]{1,0:T(8,128)(2,1)}) %all-gather.7.cloned.1.call-update) | async-done | bytes 8388624 | tf_op jit(solution)/shard_map/all_gather | solution.py:191
  133.0 5.7 %fusion.2 = bf16[256,1024]{1,0:T(8,128)(2,1)S(1)} fusion(f32[256,1024]{1,0:T(8,128)S(1)} %fusion.7, bf16[256,4096]{1,0:T(8,128)(2,1)S(1)} %bitcast.16, bf16[4096,1024]{1,0:T(8,128)(2,1)} %all-gather.7.cloned.1.call-done), kind=kOutput, calls=%fused_computation.12 | convolution fusion | flops 2148532224 | bytes 12058624 | tf_op jit(solution)/shard_map/dot_general | solution.py:20
  138.7 5.6 %convolution_convert_fusion = bf16[4096,1024]{1,0:T(8,128)(2,1)} fusion(bf16[256,4096]{1,0:T(8,128)(2,1)S(1)} %bitcast.17, bf16[256,1024]{1,0:T(8,128)(2,1)S(1)} %fusion.2), kind=kOutput, calls=%fused_computation.1 | convolution fusion | flops 2151677952 | bytes 11010048 | tf_op jit(solution)/shard_map/dot_general | solution.py:20
  144.3 0.0 reduce-scatter.3.cloned.1.call-update
  144.4 0.2 reduce-scatter.5.cloned.1.call-start
  144.6 71.2 %reduce-scatter.3.cloned.1.call-done = bf16[512,1024]{1,0:T(8,128)(2,1)} async-done(((bf16[4096,1024]{1,0:T(8,128)(2,1)}), bf16[512,1024]{1,0:T(8,128)(2,1)}) %reduce-scatter.3.cloned.1.call-update) | async-done | bytes 1048592 | tf_op jit(solution)/shard_map/reduce_scatter | solution.py:196
  215.8 0.0 copy-start.3
  215.8 11.6 %fusion.3 = f32[512,4096]{1,0:T(8,128)} fusion(bf16[4096,1024]{1,0:T(8,128)(2,1)} %all-gather.5.cloned.1.call-done, bf16[512,1024]{1,0:T(8,128)(2,1)} %reduce-scatter.3.cloned.1.call-done), kind=kOutput, calls=%fused_computation.13 | convolution fusion | flops 4296540160 | bytes 17825792 | tf_op jit(solution)/shard_map/dot_general | solution.py:20
  227.4 0.0 copy-done.3
  227.4 10.8 %add_convert_fusion = bf16[512,4096]{1,0:T(8,128)(2,1)} fusion(f32[512,4096]{1,0:T(8,128)} %fusion.3, bf16[4096,1024]{1,0:T(8,128)(2,1)} %all-gather.7.cloned.1.call-done, bf16[512,1024]{1,0:T(8,128)(2,1)S(1)} %copy-done.3), kind=kOutput, calls=%fused_computation | convolution fusion | flops 4300734464 | bytes 22020096 | tf_op jit(solution)/shard_map/dot_general | solution.py:20
  238.1 0.0 reduce-scatter.5.cloned.1.call-update
  238.2 0.0 all-gather.9.cloned.1.call-start
  238.2 76.8 %reduce-scatter.5.cloned.1.call-done = bf16[512,1024]{1,0:T(8,128)(2,1)} async-done(((bf16[512,4096]{1,0:T(8,128)(2,1)}), bf16[512,1024]{1,0:T(8,128)(2,1)}) %reduce-scatter.5.cloned.1.call-update) | async-done | bytes 1048592 | tf_op jit(solution)/shard_map/reduce_scatter | solution.py:199
  315.1 1.3 constant_dynamic-slice_fusion
  316.3 0.7 collective-permute-start
  317.0 0.1 collective-permute-start.1
  317.1 0.0 collective-permute-done
  317.1 0.2 copy.4
  317.4 1.7 collective-permute-done.1
  319.0 0.0 copy-start.1
  319.0 0.2 copy.5
  319.2 0.1 broadcast_in_dim.3
  319.4 0.1 constant_dynamic-update-slice_fusion.1
  319.4 0.1 constant_dynamic-update-slice_fusion
  319.5 0.7 copy-done.1
  320.2 2.1 multiply_reduce_fusion
  322.3 0.0 all-gather.9.cloned.1.call-update
  322.3 0.0 copy-start.2
  322.3 0.0 all-gather.11.cloned.1.call-start
  322.4 149.8 %all-gather.9.cloned.1.call-done = bf16[512,4096]{1,0:T(8,128)(2,1)} async-done(((bf16[512,1024]{1,0:T(8,128)(2,1)}), bf16[512,4096]{1,0:T(8,128)(2,1)}) %all-gather.9.cloned.1.call-update) | async-done | bytes 4194320 | tf_op jit(solution)/shard_map/all_gather | solution.py:201
  472.2 10.9 %fusion.6 = (bf16[512,1024]{1,0:T(8,128)(2,1)}, f32[512,1024]{1,0:T(8,128)}) fusion(bf16[512,4096]{1,0:T(8,128)(2,1)} %all-gather.9.cloned.1.call-done, bf16[4096,1024]{1,0:T(8,128)(2,1)} %all-gather.5.cloned.1.call-done), kind=kOutput, calls=%fused_computation.20 | convolution fusion | flops 4295491584 | bytes 15728640 | tf_op jit(solution)/shard_map/dot_general | solution.py:20
  483.1 0.0 all-gather.11.cloned.1.call-update
  483.1 39.6 %psum.7 = f32[]{:T(128)} all-reduce(f32[]{:T(128)} %get-tuple-element.5), channel_id=1, replica_groups=mesh['dp'=2,'layer'=4,'tensor'=4] {'dp','layer','tensor'}, use_global_device_ids=true, to_apply=%region_3.4 | all-reduce | flops 1 | bytes 8 | tf_op jit(solution)/shard_map/psum | solution.py:204
  523.3 13.6 %all-gather.11.cloned.1.call-done = bf16[4096,1024]{1,0:T(8,128)(2,1)} async-done(((bf16[512,1024]{1,0:T(8,128)(2,1)}), bf16[4096,1024]{1,0:T(8,128)(2,1)}) %all-gather.11.cloned.1.call-update) | async-done | bytes 8388624 | tf_op jit(solution)/shard_map/all_gather | solution.py:203
  537.0 0.0 copy-done.2
  537.0 11.0 %add_multiply_fusion = f32[512,1024]{1,0:T(8,128)} fusion(f32[512,1024]{1,0:T(8,128)} %get-tuple-element.12, f32[512,1024]{1,0:T(8,128)S(1)} %copy-done.2, bf16[512,4096]{1,0:T(8,128)(2,1)} %all-gather.9.cloned.1.call-done, bf16[4096,1024]{1,0:T(8,128)(2,1)} %all-gather.11.cloned.1.call-done, f32[]{:T(128)S(6)} %mul.53, f32[]{:T(128)S(6)} %div.19), kind=kOutput, calls=%fused_computation.5 | convolution fusion | flops 4298113024 | bytes 18874376 | tf_op jit(solution)/shard_map/dot_general | solution.py:20
Async XLA Ops:
  6.5 64.0 %all-gather.5.cloned.1.call-start = ((), (), s32[]{:S(2)}) async-start(), calls=%async_computation.2 | async-start | bytes 9437184 | tf_op jit(solution)/shard_map/all_gather | solution.py:191
  9.9 1.0 copy-start
  9.9 123.1 %all-gather.7.cloned.1.call-start = ((), (), s32[]{:S(2)}) async-start(), calls=%async_computation.3 | async-start | bytes 9437184 | tf_op jit(solution)/shard_map/all_gather | solution.py:191
  10.7 205.1 %reduce-scatter.3.cloned.1.call-start = ((), (), s32[]{:S(2)}) async-start(), calls=%async_computation.4 | async-start | bytes 9437184 | tf_op jit(solution)/shard_map/reduce_scatter | solution.py:196
  144.4 170.7 %reduce-scatter.5.cloned.1.call-start = ((), (), s32[]{:S(2)}) async-start(), calls=%async_computation.5 | async-start | bytes 5242880 | tf_op jit(solution)/shard_map/reduce_scatter | solution.py:199
  215.8 11.6 %copy-start.3 = (bf16[512,1024]{1,0:T(8,128)(2,1)S(1)}, bf16[512,1024]{1,0:T(8,128)(2,1)}, u32[]{:S(2)}) copy-start(bf16[512,1024]{1,0:T(8,128)(2,1)} %reduce-scatter.3.cloned.1.call-done) | copy-start | bytes 3145732
  238.2 234.0 %all-gather.9.cloned.1.call-start = ((), (), s32[]{:S(2)}) async-start(), calls=%async_computation.6 | async-start | bytes 5242880 | tf_op jit(solution)/shard_map/all_gather | solution.py:201
  316.3 0.8 collective-permute-start
  317.0 2.0 collective-permute-start.1
  319.0 1.2 copy-start.1
  322.3 214.6 %copy-start.2 = (f32[512,1024]{1,0:T(8,128)S(1)}, f32[512,1024]{1,0:T(8,128)}, u32[]{:S(2)}) copy-start(f32[512,1024]{1,0:T(8,128)} %param.5) | copy-start | bytes 6291460
  322.3 214.6 %all-gather.11.cloned.1.call-start = ((), (), s32[]{:S(2)}) async-start(), calls=%async_computation.7 | async-start | bytes 9437184 | tf_op jit(solution)/shard_map/all_gather | solution.py:203
Sparse Core Ops, SparseCore 0:
  10.0 60.4 all-gather.4
  72.4 60.5 all-gather.6
  144.5 71.2 reduce-scatter.2
  238.3 76.7 reduce-scatter.4
  322.4 149.6 all-gather.8
  483.2 53.6 all-gather.10

commit v2 on v1

--- a/solution.py
+++ b/solution.py
@@ -192,11 +192,17 @@
     activations = run_layers(embeddings, layer_weight)
     projected = product(activations, panel, 1, 0) + product(activations, panel_rest, 1, 0)
     cubed = projected * projected * projected
-    partial = product(activations, cubed, 0, 0).astype(HALF)
-    summed = lax.psum_scatter(partial, ROWS, scatter_dimension=0, tiled=True)
-    gradient = summed.astype(jnp.float32) / (embeddings.shape[0] * lax.axis_size("dp"))
-    cross_part = (product(gradient, panel, 1, 1) + product(gradient, panel_rest, 1, 1)).astype(HALF)
-    cross = lax.psum_scatter(cross_part, "tensor", scatter_dimension=1, tiled=True)
+    groups = lax.axis_size("dp") * lax.axis_size("layer")
+    grouped = activations.reshape(activations.shape[0], groups, 2, full_width // groups // 2)
+    crosses = []
+    for half in range(2):
+        chosen = grouped[:, :, half].reshape(activations.shape[0], full_width // 2)
+        partial = product(chosen, cubed, 0, 0).astype(HALF)
+        summed = lax.psum_scatter(partial, ROWS, scatter_dimension=0, tiled=True)
+        gradient = summed.astype(jnp.float32) / (embeddings.shape[0] * lax.axis_size("dp"))
+        cross_part = (product(gradient, panel, 1, 1) + product(gradient, panel_rest, 1, 1)).astype(HALF)
+        crosses.append(lax.psum_scatter(cross_part, "tensor", scatter_dimension=1, tiled=True))
+    cross = jnp.concatenate(crosses, axis=0)
     skew = cross.astype(jnp.float32) - transposed_block(cross).astype(jnp.float32)
     skew_rows = lax.all_gather(skew.astype(HALF), "tensor", axis=1, tiled=True)
     first_product = product(skew_rows, panel, 1, 0)

time: 555 us -> 580 us (1.045)
  local copies, waits for them, and re-layouts: 2.81 us -> 21.2 us
  matrix products: 61.3 us -> 69 us
    reduce_scatter x1 -> x2, waiting for transfers between devices: 71.2 us -> 86.7 us  [shards(): summed = lax.psum_scatter(partial, ROWS, scatter_dimension=0, tiled=True)]
    all_gather x2, waiting for transfers between devices: 79.5 us -> 64.5 us  [shards(): lax.all_gather(part, ROWS, axis=0, tiled=True)]
    unnamed x8 -> x15, local copies, waits for them, and re-layouts: 0.88 us -> 9.71 us
    dot_general x7 -> x10, matrix products: 61.3 us -> 69 us  [product(): lax.dot_general(left.astype(HALF), right.astype(HALF), dims, preferred_el...]
    slice x0 -> x1, local copies, waits for them, and re-layouts: none -> 6.88 us  [shards(): chosen = grouped[:, :, half].reshape(activations.shape[0], full_width // 2)]
    reduce_scatter x1 -> x2, waiting for transfers between devices: 76.8 us -> 76.7 us  [shards(): lax.psum_scatter(cross_part, 'tensor', scatter_dimension=1, tiled=True)]
  transfers between devices with their start and end apart: 8 -> 10, of which waited for: 7 -> 9; matrix products, arithmetic and copies ran while one was open for 1% -> 10% of each run, Pallas kernels for 7% -> 6%
where the time goes in v2:
time: 580 us
  waiting for transfers between devices  392 us (68%)
  matrix products  69 us (12%)
  blocking collectives  39.4 us (7%)
  Pallas kernels  37 us (6%)
  local copies, waits for them, and re-layouts  21.2 us (4%)
  between operations  14.4 us (2%)
    all_gather x1, waiting for transfers between devices, shards(): skew_rows = lax.all_gather(skew.astype(HALF), 'tensor', axis=1, tiled=True)  148 us
    reduce_scatter x2, waiting for transfers between devices, shards(): summed = lax.psum_scatter(partial, ROWS, scatter_dimension=0, tiled=True)  86.7 us
    reduce_scatter x2, waiting for transfers between devices, shards(): lax.psum_scatter(cross_part, 'tensor', scatter_dimension=1, tiled=True)  76.7 us
    dot_general x10, matrix products, product(): lax.dot_general(left.astype(HALF), right.astype(HALF), dims, preferred_el...  69 us
    all_gather x2, waiting for transfers between devices, shards(): lax.all_gather(part, ROWS, axis=0, tiled=True)  64.5 us
    psum x1, blocking collectives, shards(): square_total = lax.psum(jnp.sum(skew * skew), EVERY)  39.4 us
    pallas_call x1, Pallas kernels, run_layers(): pl.pallas_call(functools.partial(layers_kernel, CHUNKS), out_shape=jax.Sh...  37 us
    all_gather x1, waiting for transfers between devices, shards(): lax.all_gather(first_product.astype(HALF), ROWS, axis=0, tiled=True)  13.8 us
  transfers between devices with their start and end apart: 10, of which 9 were waited for; matrix products, arithmetic and copies ran while one was open for 10% of the time, Pallas kernels for 6%

profile of v2, /device:TPU:0, one launch (start us, length us, event | category | flops | bytes accessed | tf_op | source)
XLA Modules:
  0.0 579.7 jit_solution(1799138349349849368)
XLA Ops:
  6.5 3.4 fusion.2
  9.9 0.0 all-gather.5.cloned.1.call-update
  10.0 0.0 all-gather.7.cloned.1.call-start
  10.0 0.7 all-gather.7.cloned.1.call-update
  10.7 0.0 reduce-scatter.5.cloned.1.call-start
  10.8 37.0 %shard_map.37 = bf16[2,2,64,4096]{3,2,1,0:T(8,128)(2,1)S(1)} custom-call(bf16[128,1024]{1,0:T(8,128)(2,1)S(1)} %copy-done, bf16[2,4096,1024]{2,1,0:T(8,128)(2,1)} %weight_hbm.1), custom_call_target="tpu_custom_call" | custom-call | flops 85899345920 | bytes 335544320 | tf_op jit(solution)/shard_map/pallas_call | solution.py:142
  47.8 2.8 reshape_reshape.3
  50.6 6.9 %fusion.11 = (bf16[256,8,1,256]{3,2,1,0:T(2,128)(2,1)}, bf16[256,8,1,256]{3,2,1,0:T(2,128)(2,1)}) fusion(bf16[256,8,2,256]{3,2,1,0:T(2,128)(2,1)} %reshape_reshape.3), kind=kLoop, calls=%fused_computation.30 | loop fusion | bytes 4194304 | tf_op jit(solution)/shard_map/slice | solution.py:199
  57.5 4.5 copy.10
  62.0 8.7 %all-gather.5.cloned.1.call-done = bf16[4096,1024]{1,0:T(8,128)(2,1)} async-done(((bf16[512,1024]{1,0:T(8,128)(2,1)}), bf16[4096,1024]{1,0:T(8,128)(2,1)}) %all-gather.5.cloned.1.call-update) | async-done | bytes 8388624 | tf_op jit(solution)/shard_map/all_gather | solution.py:191
  70.6 6.7 %fusion.13 = f32[256,1024]{1,0:T(8,128)} fusion(bf16[256,4096]{1,0:T(8,128)(2,1)S(1)} %bitcast.23, bf16[4096,1024]{1,0:T(8,128)(2,1)} %all-gather.5.cloned.1.call-done), kind=kOutput, calls=%fused_computation.32 | convolution fusion | flops 2147483648 | bytes 11534336 | tf_op jit(solution)/shard_map/dot_general | solution.py:20
  77.3 55.8 %all-gather.7.cloned.1.call-done = bf16[4096,1024]{1,0:T(8,128)(2,1)} async-done(((bf16[512,1024]{1,0:T(8,128)(2,1)}), bf16[4096,1024]{1,0:T(8,128)(2,1)}) %all-gather.7.cloned.1.call-update) | async-done | bytes 8388624 | tf_op jit(solution)/shard_map/all_gather | solution.py:191
  133.1 5.9 %fusion.4 = bf16[256,1024]{1,0:T(8,128)(2,1)S(1)} fusion(f32[256,1024]{1,0:T(8,128)} %fusion.13, bf16[256,4096]{1,0:T(8,128)(2,1)S(1)} %bitcast.24, bf16[4096,1024]{1,0:T(8,128)(2,1)} %all-gather.7.cloned.1.call-done), kind=kOutput, calls=%fused_computation.15 | convolution fusion | flops 2148532224 | bytes 12058624 | tf_op jit(solution)/shard_map/dot_general | solution.py:20
  139.1 0.8 copy-done.2
  139.9 3.2 convolution_convert_fusion.1
  143.1 0.0 reduce-scatter.9.cloned.1.call-start
  143.2 1.5 copy-done.1
  144.7 1.8 copy.11
  146.5 4.3 convolution_convert_fusion
  150.8 0.2 reduce-scatter.7.cloned.1.call-start
  151.0 45.2 %reduce-scatter.5.cloned.1.call-done = bf16[256,1024]{1,0:T(8,128)(2,1)} async-done(((bf16[2048,1024]{1,0:T(8,128)(2,1)}), bf16[256,1024]{1,0:T(8,128)(2,1)}) %reduce-scatter.5.cloned.1.call-update) | async-done | bytes 524304 | tf_op jit(solution)/shard_map/reduce_scatter | solution.py:201
  196.2 6.0 %fusion.5 = f32[256,4096]{1,0:T(8,128)S(1)} fusion(bf16[4096,1024]{1,0:T(8,128)(2,1)} %all-gather.5.cloned.1.call-done, bf16[256,1024]{1,0:T(8,128)(2,1)} %reduce-scatter.5.cloned.1.call-done), kind=kOutput, calls=%fused_computation.18 | convolution fusion | flops 2148270080 | bytes 13107200 | tf_op jit(solution)/shard_map/dot_general | solution.py:20
  202.2 7.5 %fusion = bf16[256,4096]{1,0:T(8,128)(2,1)} fusion(f32[256,4096]{1,0:T(8,128)S(1)} %fusion.5, bf16[4096,1024]{1,0:T(8,128)(2,1)} %all-gather.7.cloned.1.call-done, bf16[256,1024]{1,0:T(8,128)(2,1)S(1)} %copy-done.5), kind=kOutput, calls=%fused_computation.2 | convolution fusion | flops 2150367232 | bytes 15204352 | tf_op jit(solution)/shard_map/dot_general | solution.py:20
  209.7 0.0 reduce-scatter.11.cloned.1.call-start
  209.8 41.4 %reduce-scatter.9.cloned.1.call-done = bf16[256,1024]{1,0:T(8,128)(2,1)} async-done(((bf16[2048,1024]{1,0:T(8,128)(2,1)}), bf16[256,1024]{1,0:T(8,128)(2,1)}) %reduce-scatter.9.cloned.1.call-update) | async-done | bytes 524304 | tf_op jit(solution)/shard_map/reduce_scatter | solution.py:201
  251.2 6.0 %fusion.6 = f32[256,4096]{1,0:T(8,128)S(1)} fusion(bf16[4096,1024]{1,0:T(8,128)(2,1)} %all-gather.5.cloned.1.call-done, bf16[256,1024]{1,0:T(8,128)(2,1)} %reduce-scatter.9.cloned.1.call-done), kind=kOutput, calls=%fused_computation.19 | convolution fusion | flops 2148270080 | bytes 13107200 | tf_op jit(solution)/shard_map/dot_general | solution.py:20
  257.2 7.6 %fusion.1 = bf16[256,4096]{1,0:T(8,128)(2,1)} fusion(f32[256,4096]{1,0:T(8,128)S(1)} %fusion.6, bf16[4096,1024]{1,0:T(8,128)(2,1)} %all-gather.7.cloned.1.call-done, bf16[256,1024]{1,0:T(8,128)(2,1)S(1)} %copy-done.4), kind=kOutput, calls=%fused_computation.3 | convolution fusion | flops 2150367232 | bytes 15204352 | tf_op jit(solution)/shard_map/dot_general | solution.py:20
  264.8 0.0 all-gather.9.cloned.1.call-start
  264.9 32.3 %reduce-scatter.7.cloned.1.call-done = bf16[256,1024]{1,0:T(8,128)(2,1)} async-done(((bf16[256,4096]{1,0:T(8,128)(2,1)}), bf16[256,1024]{1,0:T(8,128)(2,1)}) %reduce-scatter.7.cloned.1.call-update) | async-done | bytes 524304 | tf_op jit(solution)/shard_map/reduce_scatter | solution.py:204
  297.2 1.1 constant_dynamic-update-slice_fusion.1
  298.3 44.4 %reduce-scatter.11.cloned.1.call-done = bf16[256,1024]{1,0:T(8,128)(2,1)} async-done(((bf16[256,4096]{1,0:T(8,128)(2,1)}), bf16[256,1024]{1,0:T(8,128)(2,1)}) %reduce-scatter.11.cloned.1.call-update) | async-done | bytes 524304 | tf_op jit(solution)/shard_map/reduce_scatter | solution.py:204
  342.7 1.1 constant_dynamic-update-slice_fusion
  343.7 0.1 constant_dynamic-slice_fusion
  343.9 0.1 collective-permute-start.1
  343.9 0.7 collective-permute-start
  344.7 1.2 collective-permute-done.1
  345.8 0.2 copy.9
  346.1 0.2 copy.8
  346.3 0.1 broadcast_in_dim.3
  346.4 0.1 constant_dynamic-update-slice_fusion.3
  346.5 0.1 constant_dynamic-update-slice_fusion.2
  346.5 2.1 multiply_reduce_fusion
  348.7 0.3 all-gather.11.cloned.1.call-start
  349.0 148.1 %all-gather.9.cloned.1.call-done = bf16[512,4096]{1,0:T(8,128)(2,1)} async-done(((bf16[512,1024]{1,0:T(8,128)(2,1)}), bf16[512,4096]{1,0:T(8,128)(2,1)}) %all-gather.9.cloned.1.call-update) | async-done | bytes 4194320 | tf_op jit(solution)/shard_map/all_gather | solution.py:207
  497.1 10.9 %fusion.12 = (bf16[512,1024]{1,0:T(8,128)(2,1)}, f32[512,1024]{1,0:T(8,128)}) fusion(bf16[512,4096]{1,0:T(8,128)(2,1)} %all-gather.9.cloned.1.call-done, bf16[4096,1024]{1,0:T(8,128)(2,1)} %all-gather.5.cloned.1.call-done), kind=kOutput, calls=%fused_computation.31 | convolution fusion | flops 4295491584 | bytes 15728640 | tf_op jit(solution)/shard_map/dot_general | solution.py:20
  508.0 39.4 %psum.7 = f32[]{:T(128)} all-reduce(f32[]{:T(128)} %get-tuple-element.5), channel_id=1, replica_groups=mesh['dp'=2,'layer'=4,'tensor'=4] {'dp','layer','tensor'}, use_global_device_ids=true, to_apply=%region_5.6 | all-reduce | flops 1 | bytes 8 | tf_op jit(solution)/shard_map/psum | solution.py:210
  548.1 13.8 %all-gather.11.cloned.1.call-done = bf16[4096,1024]{1,0:T(8,128)(2,1)} async-done(((bf16[512,1024]{1,0:T(8,128)(2,1)}), bf16[4096,1024]{1,0:T(8,128)(2,1)}) %all-gather.11.cloned.1.call-update) | async-done | bytes 8388624 | tf_op jit(solution)/shard_map/all_gather | solution.py:209
  561.9 11.0 %add_multiply_fusion = f32[512,1024]{1,0:T(8,128)} fusion(f32[512,1024]{1,0:T(8,128)} %get-tuple-element.14, f32[512,1024]{1,0:T(8,128)S(1)} %copy-done.3, bf16[512,4096]{1,0:T(8,128)(2,1)} %all-gather.9.cloned.1.call-done, bf16[4096,1024]{1,0:T(8,128)(2,1)} %all-gather.11.cloned.1.call-done, f32[]{:T(128)S(6)} %mul.53, f32[]{:T(128)S(6)} %div.19), kind=kOutput, calls=%fused_computation.9 | convolution fusion | flops 4298113024 | bytes 18874376 | tf_op jit(solution)/shard_map/dot_general | solution.py:20
  (18 shorter events, 0.1 us)
Async XLA Ops:
  6.5 4.2 copy-start
  6.5 64.1 %all-gather.5.cloned.1.call-start = ((), (), s32[]{:S(2)}) async-start(), calls=%async_computation.4 | async-start | bytes 9437184 | tf_op jit(solution)/shard_map/all_gather | solution.py:191
  10.0 123.2 %all-gather.7.cloned.1.call-start = ((), (), s32[]{:S(2)}) async-start(), calls=%async_computation.5 | async-start | bytes 9437184 | tf_op jit(solution)/shard_map/all_gather | solution.py:191
  10.7 185.5 %reduce-scatter.5.cloned.1.call-start = ((), (), s32[]{:S(2)}) async-start(), calls=%async_computation.6 | async-start | bytes 4718592 | tf_op jit(solution)/shard_map/reduce_scatter | solution.py:201
  139.1 0.8 copy-start.2
  143.1 1.6 copy-start.1
  143.1 108.1 %reduce-scatter.9.cloned.1.call-start = ((), (), s32[]{:S(2)}) async-start(), calls=%async_computation.8 | async-start | bytes 4718592 | tf_op jit(solution)/shard_map/reduce_scatter | solution.py:201
  150.8 146.4 %reduce-scatter.7.cloned.1.call-start = ((), (), s32[]{:S(2)}) async-start(), calls=%async_computation.7 | async-start | bytes 2621440 | tf_op jit(solution)/shard_map/reduce_scatter | solution.py:204
  196.2 6.0 %copy-start.5 = (bf16[256,1024]{1,0:T(8,128)(2,1)S(1)}, bf16[256,1024]{1,0:T(8,128)(2,1)}, u32[]{:S(2)}) copy-start(bf16[256,1024]{1,0:T(8,128)(2,1)} %reduce-scatter.5.cloned.1.call-done) | copy-start | bytes 1572868
  209.7 133.0 %reduce-scatter.11.cloned.1.call-start = ((), (), s32[]{:S(2)}) async-start(), calls=%async_computation.9 | async-start | bytes 2621440 | tf_op jit(solution)/shard_map/reduce_scatter | solution.py:204
  251.2 6.0 %copy-start.4 = (bf16[256,1024]{1,0:T(8,128)(2,1)S(1)}, bf16[256,1024]{1,0:T(8,128)(2,1)}, u32[]{:S(2)}) copy-start(bf16[256,1024]{1,0:T(8,128)(2,1)} %reduce-scatter.9.cloned.1.call-done) | copy-start | bytes 1572868
  264.8 232.3 %all-gather.9.cloned.1.call-start = ((), (), s32[]{:S(2)}) async-start(), calls=%async_computation.10 | async-start | bytes 5242880 | tf_op jit(solution)/shard_map/all_gather | solution.py:207
  343.9 2.0 collective-permute-start.1
  343.9 2.1 collective-permute-start
  348.7 213.2 %copy-start.3 = (f32[512,1024]{1,0:T(8,128)S(1)}, f32[512,1024]{1,0:T(8,128)}, u32[]{:S(2)}) copy-start(f32[512,1024]{1,0:T(8,128)} %param.5) | copy-start | bytes 6291460
  348.7 213.2 %all-gather.11.cloned.1.call-start = ((), (), s32[]{:S(2)}) async-start(), calls=%async_computation.11 | async-start | bytes 9437184 | tf_op jit(solution)/shard_map/all_gather | solution.py:209
Sparse Core Ops, SparseCore 0:
  10.1 60.5 all-gather.4
  72.5 60.5 all-gather.6
  143.2 52.9 reduce-scatter.4
  199.8 51.3 reduce-scatter.8
  253.3 43.8 reduce-scatter.6
  299.5 43.1 reduce-scatter.10
  348.8 148.2 all-gather.8
  508.1 53.6 all-gather.10

commit v3 on v1

--- a/solution.py
+++ b/solution.py
@@ -184,6 +184,17 @@
     return result
 
 
+def gathered_columns(block):
+    count, me, width = lax.axis_size("tensor"), lax.axis_index("tensor"), block.shape[1]
+    result = jnp.zeros((block.shape[0], count * width), block.dtype)
+    for turn in range(count):
+        got = block
+        if turn:
+            got = lax.ppermute(block, "tensor", [(t, (t + turn) % count) for t in range(count)])
+        result = lax.dynamic_update_slice_in_dim(result, got, ((me + count - turn) % count) * width, 1)
+    return result
+
+
 def shards(embeddings, layer_weight, rotation):
     full_width = layer_weight.shape[1]
     root_width = math.sqrt(full_width)
@@ -198,7 +209,7 @@
     cross_part = (product(gradient, panel, 1, 1) + product(gradient, panel_rest, 1, 1)).astype(HALF)
     cross = lax.psum_scatter(cross_part, "tensor", scatter_dimension=1, tiled=True)
     skew = cross.astype(jnp.float32) - transposed_block(cross).astype(jnp.float32)
-    skew_rows = lax.all_gather(skew.astype(HALF), "tensor", axis=1, tiled=True)
+    skew_rows = gathered_columns(skew.astype(HALF))
     first_product = product(skew_rows, panel, 1, 0)
     product_panel = lax.all_gather(first_product.astype(HALF), ROWS, axis=0, tiled=True)
     square_total = lax.psum(jnp.sum(skew * skew), EVERY)

time: 555 us -> 594 us (1.070)
  starting transfers between devices: 1.15 us -> 95.5 us
  waiting for transfers between devices: 393 us -> 302 us
  blocking collectives: 39.6 us -> 65.5 us
  local copies, waits for them, and re-layouts: 2.81 us -> 11.4 us
    all_gather x1 -> x0, waiting for transfers between devices: 150 us -> none  [shards(): skew_rows = lax.all_gather(skew.astype(HALF), 'tensor', axis=1, tiled=True)]
    ppermute x0 -> x3, starting transfers between devices: none -> 94.4 us  [gathered_columns(): lax.ppermute(block, 'tensor', [(t, (t + turn) % count) for t in range(cou...]
    ppermute x0 -> x3, waiting for transfers between devices: none -> 59.7 us  [gathered_columns(): lax.ppermute(block, 'tensor', [(t, (t + turn) % count) for t in range(cou...]
    psum x1, blocking collectives: 39.6 us -> 65.5 us  [shards(): square_total = lax.psum(jnp.sum(skew * skew), EVERY)]
    dynamic_update_slice x0 -> x3, local copies, waits for them, and re-layouts: none -> 6.96 us  [gathered_columns(): lax.dynamic_update_slice_in_dim(result, got, (me + count - turn) % count...]
  transfers between devices with their start and end apart: 8 -> 10, of which waited for: 7 -> 9; matrix products, arithmetic and copies ran while one was open for 1% -> 2% of each run, Pallas kernels for 7% -> 6%
where the time goes in v3:
time: 594 us
  waiting for transfers between devices  302 us (51%)
  starting transfers between devices  95.5 us (16%)
  blocking collectives  65.5 us (11%)
  matrix products  61.8 us (10%)
  Pallas kernels  37 us (6%)
  between operations  14 us (2%)
  local copies, waits for them, and re-layouts  11.4 us (2%)
  other arithmetic  6.19 us (1%)
    ppermute x3, starting transfers between devices, gathered_columns(): lax.ppermute(block, 'tensor', [(t, (t + turn) % count) for t in range(cou...  94.4 us
    all_gather x2, waiting for transfers between devices, shards(): lax.all_gather(part, ROWS, axis=0, tiled=True)  79.6 us
    reduce_scatter x1, waiting for transfers between devices, shards(): lax.psum_scatter(cross_part, 'tensor', scatter_dimension=1, tiled=True)  76.8 us
    reduce_scatter x1, waiting for transfers between devices, shards(): summed = lax.psum_scatter(partial, ROWS, scatter_dimension=0, tiled=True)  71.2 us
    psum x1, blocking collectives, shards(): square_total = lax.psum(jnp.sum(skew * skew), EVERY)  65.5 us
    dot_general x7, matrix products, product(): lax.dot_general(left.astype(HALF), right.astype(HALF), dims, preferred_el...  61.8 us
    ppermute x3, waiting for transfers between devices, gathered_columns(): lax.ppermute(block, 'tensor', [(t, (t + turn) % count) for t in range(cou...  59.7 us
    pallas_call x1, Pallas kernels, run_layers(): pl.pallas_call(functools.partial(layers_kernel, CHUNKS), out_shape=jax.Sh...  37 us
  transfers between devices with their start and end apart: 10, of which 9 were waited for; matrix products, arithmetic and copies ran while one was open for 2% of the time, Pallas kernels for 6%

profile of v3, /device:TPU:0, one launch (start us, length us, event | category | flops | bytes accessed | tf_op | source)
XLA Modules:
  0.0 593.5 jit_solution(17353048128762539080)
XLA Ops:
  6.5 0.0 all-gather.4.cloned.1.call-start
  6.5 3.4 fusion
  9.9 0.0 all-gather.4.cloned.1.call-update
  10.0 0.0 all-gather.6.cloned.1.call-start
  10.0 0.7 all-gather.6.cloned.1.call-update
  10.7 0.0 reduce-scatter.3.cloned.1.call-start
  10.8 37.0 %shard_map.37 = bf16[2,2,64,4096]{3,2,1,0:T(8,128)(2,1)S(1)} custom-call(bf16[128,1024]{1,0:T(8,128)(2,1)S(1)} %copy-done, bf16[2,4096,1024]{2,1,0:T(8,128)(2,1)} %weight_hbm.1), custom_call_target="tpu_custom_call" | custom-call | flops 85899345920 | bytes 335544320 | tf_op jit(solution)/shard_map/pallas_call | solution.py:142
  47.8 22.8 %all-gather.4.cloned.1.call-done = bf16[4096,1024]{1,0:T(8,128)(2,1)} async-done(((bf16[512,1024]{1,0:T(8,128)(2,1)}), bf16[4096,1024]{1,0:T(8,128)(2,1)}) %all-gather.4.cloned.1.call-update) | async-done | bytes 8388624 | tf_op jit(solution)/shard_map/all_gather | solution.py:202
  70.6 5.7 fusion.8
  76.3 56.8 %all-gather.6.cloned.1.call-done = bf16[4096,1024]{1,0:T(8,128)(2,1)} async-done(((bf16[512,1024]{1,0:T(8,128)(2,1)}), bf16[4096,1024]{1,0:T(8,128)(2,1)}) %all-gather.6.cloned.1.call-update) | async-done | bytes 8388624 | tf_op jit(solution)/shard_map/all_gather | solution.py:202
  133.1 5.7 fusion.2
  138.8 5.6 convolution_convert_fusion
  144.5 0.0 reduce-scatter.3.cloned.1.call-update
  144.5 0.2 reduce-scatter.5.cloned.1.call-start
  144.7 71.2 %reduce-scatter.3.cloned.1.call-done = bf16[512,1024]{1,0:T(8,128)(2,1)} async-done(((bf16[4096,1024]{1,0:T(8,128)(2,1)}), bf16[512,1024]{1,0:T(8,128)(2,1)}) %reduce-scatter.3.cloned.1.call-update) | async-done | bytes 1048592 | tf_op jit(solution)/shard_map/reduce_scatter | solution.py:207
  215.9 11.5 %fusion.3 = f32[512,4096]{1,0:T(8,128)} fusion(bf16[4096,1024]{1,0:T(8,128)(2,1)} %all-gather.4.cloned.1.call-done, bf16[512,1024]{1,0:T(8,128)(2,1)} %reduce-scatter.3.cloned.1.call-done), kind=kOutput, calls=%fused_computation.13 | convolution fusion | flops 4296540160 | bytes 17825792 | tf_op jit(solution)/shard_map/dot_general | solution.py:20
  227.5 0.0 copy-done.2
  227.5 10.7 %add_convert_fusion = bf16[512,4096]{1,0:T(8,128)(2,1)} fusion(f32[512,4096]{1,0:T(8,128)} %fusion.3, bf16[4096,1024]{1,0:T(8,128)(2,1)} %all-gather.6.cloned.1.call-done, bf16[512,1024]{1,0:T(8,128)(2,1)S(1)} %copy-done.2), kind=kOutput, calls=%fused_computation | convolution fusion | flops 4300734464 | bytes 22020096 | tf_op jit(solution)/shard_map/dot_general | solution.py:20
  238.2 0.0 reduce-scatter.5.cloned.1.call-update
  238.2 0.0 all-gather.8.cloned.1.call-start
  238.3 76.8 %reduce-scatter.5.cloned.1.call-done = bf16[512,1024]{1,0:T(8,128)(2,1)} async-done(((bf16[512,4096]{1,0:T(8,128)(2,1)}), bf16[512,1024]{1,0:T(8,128)(2,1)}) %reduce-scatter.5.cloned.1.call-update) | async-done | bytes 1048592 | tf_op jit(solution)/shard_map/reduce_scatter | solution.py:210
  315.2 1.3 constant_dynamic-slice_fusion
  316.4 0.7 collective-permute-start
  317.1 0.1 collective-permute-start.1
  317.2 0.0 collective-permute-done
  317.2 0.2 copy.4
  317.5 1.6 collective-permute-done.1
  319.1 0.2 copy.5
  319.3 0.1 broadcast_in_dim.6
  319.4 0.1 constant_dynamic-update-slice_fusion.5
  319.5 0.1 constant_dynamic-update-slice_fusion.4
  319.6 2.5 broadcast_in_dim.7
  322.1 1.6 constant_dynamic-update-slice_fusion.3
  323.7 92.0 %collective-permute-start.2 = (bf16[512,1024]{1,0:T(8,128)(2,1)S(1)}, bf16[512,1024]{1,0:T(8,128)(2,1)}, u32[]{:S(2)}, u32[]{:S(2)}) collective-permute-start(bf16[512,1024]{1,0:T(8,128)(2,1)S(1)} %get-tuple-element.6), channel_id=1, source_target_pairs={{0,1},{1,2},{2,3},{3,0},{4,5},{5,6},{6,7},{7,4},{8,9},{9,10},{10,1... | collective-permute-start | bytes 3145736 | tf_op jit(solution)/shard_map/ppermute | solution.py:193
  415.7 0.0 collective-permute-start.3
  415.7 2.4 collective-permute-start.4
  418.0 21.2 %collective-permute-done.2 = bf16[512,1024]{1,0:T(8,128)(2,1)} collective-permute-done((bf16[512,1024]{1,0:T(8,128)(2,1)S(1)}, bf16[512,1024]{1,0:T(8,128)(2,1)}, u32[]{:S(2)}, u32[]{:S(2)}) %collective-permute-start.2) | collective-permute-done | bytes 1048608 | tf_op jit(solution)/shard_map/ppermute | solution.py:193
  439.3 2.3 constant_dynamic-update-slice_fusion.2
  441.6 21.2 %collective-permute-done.3 = bf16[512,1024]{1,0:T(8,128)(2,1)} collective-permute-done((bf16[512,1024]{1,0:T(8,128)(2,1)S(1)}, bf16[512,1024]{1,0:T(8,128)(2,1)}, u32[]{:S(2)}, u32[]{:S(2)}) %collective-permute-start.3) | collective-permute-done | bytes 1048608 | tf_op jit(solution)/shard_map/ppermute | solution.py:193
  462.9 2.3 constant_dynamic-update-slice_fusion.1
  465.1 17.2 %collective-permute-done.4 = bf16[512,1024]{1,0:T(8,128)(2,1)} collective-permute-done((bf16[512,1024]{1,0:T(8,128)(2,1)S(1)}, bf16[512,1024]{1,0:T(8,128)(2,1)}, u32[]{:S(2)}, u32[]{:S(2)}) %collective-permute-start.4) | collective-permute-done | bytes 1048608 | tf_op jit(solution)/shard_map/ppermute | solution.py:193
  482.4 2.4 constant_dynamic-update-slice_fusion
  484.7 10.9 %fusion.7 = (bf16[512,1024]{1,0:T(8,128)(2,1)}, f32[512,1024]{1,0:T(8,128)}) fusion(bf16[512,4096]{1,0:T(8,128)(2,1)} %constant_dynamic-update-slice_fusion, bf16[4096,1024]{1,0:T(8,128)(2,1)} %all-gather.4.cloned.1.call-done), kind=kOutput, calls=%fused_computation.24 | convolution fusion | flops 4295491584 | bytes 15728640 | tf_op jit(solution)/shard_map/dot_general | solution.py:20
  495.6 0.0 all-gather.8.cloned.1.call-update
  495.6 1.2 multiply_reduce_fusion
  496.9 65.5 %psum.7 = f32[]{:T(128)} all-reduce(f32[]{:T(128)} %multiply_reduce_fusion), channel_id=1, replica_groups=mesh['dp'=2,'layer'=4,'tensor'=4] {'dp','layer','tensor'}, use_global_device_ids=true, to_apply=%region_3.4 | all-reduce | flops 1 | bytes 8 | tf_op jit(solution)/shard_map/psum | solution.py:215
  563.0 12.3 %all-gather.8.cloned.1.call-done = bf16[4096,1024]{1,0:T(8,128)(2,1)} async-done(((bf16[512,1024]{1,0:T(8,128)(2,1)}), bf16[4096,1024]{1,0:T(8,128)(2,1)}) %all-gather.8.cloned.1.call-update) | async-done | bytes 8388624 | tf_op jit(solution)/shard_map/all_gather | solution.py:214
  575.4 11.6 %add_multiply_fusion = f32[512,1024]{1,0:T(8,128)} fusion(f32[512,1024]{1,0:T(8,128)} %get-tuple-element.12, f32[512,1024]{1,0:T(8,128)} %param.5, bf16[512,4096]{1,0:T(8,128)(2,1)} %constant_dynamic-update-slice_fusion, bf16[4096,1024]{1,0:T(8,128)(2,1)} %all-gather.8.cloned.1.call-done, f32[]{:T(128)S(6)} %mul.69, f32[]{:T(128)S(6)} %div.19), kind=kOutput, calls=%fused_computation.5 | convolution fusion | flops 4298113024 | bytes 18874376 | tf_op jit(solution)/shard_map/dot_general | solution.py:20
  (5 shorter events, 0.0 us)
Async XLA Ops:
  6.5 4.2 copy-start
  6.5 64.1 %all-gather.4.cloned.1.call-start = ((), (), s32[]{:S(2)}) async-start(), calls=%async_computation.2 | async-start | bytes 9437184 | tf_op jit(solution)/shard_map/all_gather | solution.py:202
  10.0 123.2 %all-gather.6.cloned.1.call-start = ((), (), s32[]{:S(2)}) async-start(), calls=%async_computation.3 | async-start | bytes 9437184 | tf_op jit(solution)/shard_map/all_gather | solution.py:202
  10.7 205.2 %reduce-scatter.3.cloned.1.call-start = ((), (), s32[]{:S(2)}) async-start(), calls=%async_computation.4 | async-start | bytes 9437184 | tf_op jit(solution)/shard_map/reduce_scatter | solution.py:207
  144.5 170.7 %reduce-scatter.5.cloned.1.call-start = ((), (), s32[]{:S(2)}) async-start(), calls=%async_computation.5 | async-start | bytes 5242880 | tf_op jit(solution)/shard_map/reduce_scatter | solution.py:210
  215.9 11.6 %copy-start.2 = (bf16[512,1024]{1,0:T(8,128)(2,1)S(1)}, bf16[512,1024]{1,0:T(8,128)(2,1)}, u32[]{:S(2)}) copy-start(bf16[512,1024]{1,0:T(8,128)(2,1)} %reduce-scatter.3.cloned.1.call-done) | copy-start | bytes 3145732
  238.2 337.1 %all-gather.8.cloned.1.call-start = ((), (), s32[]{:S(2)}) async-start(), calls=%async_computation.6 | async-start | bytes 9437184 | tf_op jit(solution)/shard_map/all_gather | solution.py:214
  316.4 0.8 collective-permute-start
  317.1 2.0 collective-permute-start.1
  319.1 3.0 copy-start.1
  323.7 115.6 %collective-permute-start.2 = (bf16[512,1024]{1,0:T(8,128)(2,1)S(1)}, bf16[512,1024]{1,0:T(8,128)(2,1)}, u32[]{:S(2)}, u32[]{:S(2)}) collective-permute-start(bf16[512,1024]{1,0:T(8,128)(2,1)S(1)} %get-tuple-element.6), channel_id=1, source_target_pairs={{0,1},{1,2},{2,3},{3,0},{4,5},{5,6},{6,7},{7,4},{8,9},{9,10},{10,1... | collective-permute-start | bytes 3145736 | tf_op jit(solution)/shard_map/ppermute | solution.py:193
  415.7 47.2 %collective-permute-start.3 = (bf16[512,1024]{1,0:T(8,128)(2,1)S(1)}, bf16[512,1024]{1,0:T(8,128)(2,1)}, u32[]{:S(2)}, u32[]{:S(2)}) collective-permute-start(bf16[512,1024]{1,0:T(8,128)(2,1)S(1)} %get-tuple-element.6), channel_id=1, source_target_pairs={{0,2},{1,3},{2,0},{3,1},{4,6},{5,7},{6,4},{7,5},{8,10},{9,11},{10,... | collective-permute-start | bytes 3145736 | tf_op jit(solution)/shard_map/ppermute | solution.py:193
  415.7 66.7 %collective-permute-start.4 = (bf16[512,1024]{1,0:T(8,128)(2,1)S(1)}, bf16[512,1024]{1,0:T(8,128)(2,1)}, u32[]{:S(2)}, u32[]{:S(2)}) collective-permute-start(bf16[512,1024]{1,0:T(8,128)(2,1)S(1)} %get-tuple-element.6), channel_id=1, source_target_pairs={{0,3},{1,0},{2,1},{3,2},{4,7},{5,4},{6,5},{7,6},{8,11},{9,8},{10,9... | collective-permute-start | bytes 3145736 | tf_op jit(solution)/shard_map/ppermute | solution.py:193
Sparse Core Ops, SparseCore 0:
  10.1 60.5 all-gather.3
  72.5 60.5 all-gather.5
  144.6 71.2 reduce-scatter.2
  238.4 76.7 reduce-scatter.4
  495.7 79.5 all-gather.7
